TPU v7x, 128 devices: a whole 4x4x4 slice. The times are simulated.
128 devices in a mesh: leaf: 4 (over y), rows: 32 (over z, x, core).
Axes of the slice: x: 4, y: 4, z: 4, core: 2. Of those that a mesh axis runs over, the one named last changes fastest.
Arguments:
- leaf_rhs: float32 [8, 16, 2048], P(None, 'leaf', 'rows'), may hold values from -6 to 6
- parent_rhs: float32 [8, 4, 4096], P(None, 'leaf', 'rows'), may hold values from -6 to 6
- root_rhs: float32 [8, 4096], P(None, ('leaf', 'rows')), may hold values from -6 to 6
- leaf_inv: bfloat16 [16, 2048, 2048], P('leaf', 'rows'), as said below
- leaf_panel: bfloat16 [16, 8192, 2048], P('leaf', 'rows'), may hold values from -0.0625 to 0.0625
- leaf_rows: int32 [16, 8192], P('leaf', 'rows'), may hold values from 0 to 8191, as said below
- leaf_height: int32 [16], P('leaf'), may hold values from 2048 to 8192
- parent_inv: bfloat16 [4, 4096, 4096], P('leaf', 'rows'), as said below
- parent_panel: bfloat16 [4, 4096, 4096], P('leaf', 'rows'), may hold values from -0.046875 to 0.046875
- parent_rows: int32 [4, 4096], P('leaf', 'rows'), may hold values from 0 to 4095, as said below
- parent_height: int32 [4], P('leaf'), may hold values from 1024 to 4096
- root_inv: bfloat16 [4096, 4096], P('rows'), as said below
Outputs:
- leaf_solution: float32 [8, 16, 2048], P(None, 'leaf', 'rows')
- parent_solution: float32 [8, 4, 4096], P(None, 'leaf', 'rows')
- root_solution: float32 [8, 4096], P(None, ('leaf', 'rows'))
Inputs may be any that keep to these rules, and one draw needn't show every extreme that they name: `leaf_rows`: each leaf's first leaf_height entries are distinct and ascending; every entry is a valid ancestor index. `parent_rows`: each parent's first parent_height entries are distinct and ascending. `leaf_inv`: A dense well conditioned matrix. `parent_inv`: A dense well conditioned matrix. `root_inv`: A dense well conditioned matrix.
All inputs are finite; a program needn't handle non-finite values.
Results may differ from a plain program's by a relative error of at most 0.009.
Values may be sent and summed in bfloat16 or wider, within the bound.
A program may use at most 64 MiB of HBM per device.

v0:
```python
import jax
import jax.numpy as jnp
from jax import lax
from jax.sharding import PartitionSpec as P


def shards(
    leaf_rhs,
    parent_rhs,
    root_rhs,
    leaf_inv,
    leaf_panel,
    leaf_rows,
    leaf_height,
    parent_inv,
    parent_panel,
    parent_rows,
    parent_height,
    root_inv,
):
    rcount = leaf_rhs.shape[0]
    group_leaves = leaf_rhs.shape[1]
    leaf_local = leaf_panel.shape[1]
    parent_width = parent_inv.shape[2]
    root_width = root_inv.shape[1]
    row_index = lax.axis_index("rows")
    parent_cols = parent_rhs.shape[2]
    root_cols = root_rhs.shape[1]
    flat_index = lax.axis_index("leaf") * lax.axis_size("rows") + row_index
    block = leaf_inv
    ly = jnp.einsum(
        "rln,lin->rli",
        lax.all_gather(leaf_rhs.astype(jnp.bfloat16), "rows", axis=2, tiled=True),
        block,
        preferred_element_type=jnp.float32,
    )
    lyb = ly.astype(jnp.bfloat16)
    block = leaf_panel
    lupd = jnp.einsum(
        "rln,lhn->rlh",
        lax.all_gather(lyb, "rows", axis=2, tiled=True),
        block,
        preferred_element_type=jnp.float32,
    )
    leaf_pos = row_index * leaf_local + jnp.arange(leaf_local, dtype=jnp.int32)
    leaf_mask = leaf_pos[None, :] < leaf_height[:, None]
    lupd = jnp.where(leaf_mask[None, :, :], lupd, 0.0)
    leaf_flat = leaf_rows.reshape(-1)
    local_acc = (
        jnp.zeros((rcount, parent_width + root_width), jnp.float32)
        .at[:, leaf_flat]
        .add(lupd.reshape(rcount, -1))
    )
    group_acc = lax.psum(local_acc, "rows")
    parent_acc = group_acc[:, :parent_width]
    root_from_leaves = lax.psum(group_acc[:, parent_width:], "leaf")
    parent_slice = lax.dynamic_slice_in_dim(parent_acc, row_index * parent_cols, parent_cols, 1)
    prb = (parent_rhs[:, 0, :] - parent_slice).astype(jnp.bfloat16)
    inverse_rows = parent_inv[0]
    panel_rows = parent_panel[0]
    block = inverse_rows
    py = jnp.dot(
        lax.all_gather(prb, "rows", axis=1, tiled=True), block.T, preferred_element_type=jnp.float32
    )
    pyb = py.astype(jnp.bfloat16)
    parent_local = panel_rows.shape[0]
    block = panel_rows
    pupd = jnp.dot(
        lax.all_gather(pyb, "rows", axis=1, tiled=True), block.T, preferred_element_type=jnp.float32
    )
    parent_pos = row_index * parent_local + jnp.arange(parent_local, dtype=jnp.int32)
    parent_mask = parent_pos < parent_height[0]
    pupd = jnp.where(parent_mask[None, :], pupd, 0.0)
    parent_root = jnp.zeros((rcount, root_width), jnp.float32).at[:, parent_rows[0]].add(pupd)
    root_acc = root_from_leaves + lax.psum(parent_root, ("leaf", "rows"))
    root_slice = lax.dynamic_slice_in_dim(root_acc, flat_index * root_cols, root_cols, 1)
    rrb = (root_rhs - root_slice).astype(jnp.bfloat16)
    block = root_inv
    ry = jnp.dot(
        lax.all_gather(rrb, ("leaf", "rows"), axis=1, tiled=True),
        block.T,
        preferred_element_type=jnp.float32,
    )
    root_term = jnp.dot(ry.astype(jnp.bfloat16), root_inv, preferred_element_type=jnp.float32)
    root_full = lax.psum(root_term, "rows")
    root_solution = lax.dynamic_slice_in_dim(root_full, flat_index * root_cols, root_cols, 1)
    rxb = root_full.astype(jnp.bfloat16)
    parent_anc = rxb[:, parent_rows[0]]
    parent_anc = jnp.where(parent_mask[None, :], parent_anc, jnp.zeros_like(parent_anc))
    parent_term = jnp.dot(parent_anc, panel_rows, preferred_element_type=jnp.float32)
    parent_tail = lax.psum_scatter(parent_term, "rows", scatter_dimension=1, tiled=True)
    pvb = (py - parent_tail).astype(jnp.bfloat16)
    parent_sol_term = jnp.dot(pvb, inverse_rows, preferred_element_type=jnp.float32)
    parent_sol = lax.psum_scatter(parent_sol_term, "rows", scatter_dimension=1, tiled=True)
    parent_whole = lax.all_gather(parent_sol.astype(jnp.bfloat16), "rows", axis=1, tiled=True)
    ancestors = jnp.concatenate([parent_whole, rxb], axis=1)
    leaf_anc = ancestors[:, leaf_flat].reshape(rcount, group_leaves, leaf_local)
    leaf_anc = jnp.where(leaf_mask[None, :, :], leaf_anc, jnp.zeros_like(leaf_anc))
    leaf_term = jnp.einsum("rlh,lhc->rlc", leaf_anc, leaf_panel, preferred_element_type=jnp.float32)
    leaf_tail = lax.psum_scatter(leaf_term, "rows", scatter_dimension=2, tiled=True)
    lvb = (ly - leaf_tail).astype(jnp.bfloat16)
    leaf_sol_term = jnp.einsum("rli,lic->rlc", lvb, leaf_inv, preferred_element_type=jnp.float32)
    leaf_sol = lax.psum_scatter(leaf_sol_term, "rows", scatter_dimension=2, tiled=True)
    return (leaf_sol, parent_sol[:, None, :], root_solution)


def solution(mesh):
    return jax.shard_map(
        shards,
        mesh=mesh,
        in_specs=(
            P(None, "leaf", "rows"),
            P(None, "leaf", "rows"),
            P(None, ("leaf", "rows")),
            P("leaf", "rows", None),
            P("leaf", "rows", None),
            P("leaf", "rows"),
            P("leaf"),
            P("leaf", "rows", None),
            P("leaf", "rows", None),
            P("leaf", "rows"),
            P("leaf"),
            P("rows", None),
        ),
        out_specs=(P(None, "leaf", "rows"), P(None, "leaf", "rows"), P(None, ("leaf", "rows"))),
        check_vma=False,
    )
```

profile of v0, /device:TPU:0, one launch (start us, length us, event | category | flops | bytes accessed | tf_op | source)
XLA Modules:
  0.0 916.0 jit_solution(10626270217796478974)
XLA Ops:
  7.2 0.0 all-reduce.5.cloned.1.call-start
  7.2 0.8 copy.81
  8.0 0.7 copy.91
  8.7 0.1 copy.62
  8.9 27.5 %all_gather.18 = bf16[8,4,2048]{0,1,2:T(4,128)(2,1)S(1)} all-gather(bf16[8,4,64]{0,1,2:T(4,128)(2,1)S(1)} %copy.62), channel_id=1, replica_groups=mesh['leaf'=4,'rows'=32] {'rows'}, dimensions={2}, use_global_device_ids=true | all-gather | bytes 135168 | tf_op jit(solution)/shard_map/all_gather | solution.py:33
  36.4 0.8 fusion.36
  37.1 0.1 copy.64
  37.3 25.3 %all_gather.19 = bf16[8,4,2048]{0,1,2:T(4,128)(2,1)S(1)} all-gather(bf16[8,4,64]{0,1,2:T(4,128)(2,1)S(1)} %copy.64), channel_id=1, replica_groups=mesh['leaf'=4,'rows'=32] {'rows'}, dimensions={2}, use_global_device_ids=true | all-gather | bytes 135168 | tf_op jit(solution)/shard_map/all_gather | solution.py:41
  62.6 0.1 broadcast_compare_fusion
  62.7 3.4 fusion.6
  66.1 0.2 copy.66
  66.3 8.2 scatter_custom_fusion
  74.5 3.5 copy.67
  78.0 0.0 all-reduce.5.cloned.1.call-update
  78.1 0.0 all-reduce.9.cloned.1.call-start
  78.9 100.7 %all-reduce.5.cloned.1.call-done = f32[8,8192]{1,0:T(8,128)} async-done(((f32[8,8192]{1,0:T(8,128)}), f32[8,8192]{1,0:T(8,128)}) %all-reduce.5.cloned.1.call-update) | async-done | bytes 262160 | tf_op jit(solution)/shard_map/psum | solution.py:54
  179.6 1.6 fusion.35
  181.2 24.6 %all_gather.20 = bf16[8,4096]{1,0:T(8,128)(2,1)S(1)} all-gather(bf16[8,128]{1,0:T(8,128)(2,1)S(1)} %subtract_convert_fusion.3), channel_id=1, replica_groups=mesh['leaf'=4,'rows'=32] {'rows'}, dimensions={1}, use_global_device_ids=true | all-gather | bytes 67584 | tf_op jit(solution)/shard_map/all_gather | solution.py:63
  205.9 0.4 fusion.37
  206.2 21.5 %all_gather.21 = bf16[8,4096]{1,0:T(8,128)(2,1)S(1)} all-gather(bf16[8,128]{1,0:T(8,128)(2,1)S(1)} %get-tuple-element.22), channel_id=1, replica_groups=mesh['leaf'=4,'rows'=32] {'rows'}, dimensions={1}, use_global_device_ids=true | all-gather | bytes 67584 | tf_op jit(solution)/shard_map/all_gather | solution.py:69
  227.8 0.4 fusion.12
  228.1 0.1 copy.68
  228.3 1.5 scatter_custom_fusion.1
  229.8 1.2 copy.69
  231.0 0.0 all-reduce.7.cloned.1.call-start
  231.1 0.7 all-reduce.7.cloned.1.call-update
  231.8 0.0 all-reduce.11.cloned.1.call-start
  231.8 141.0 %all-reduce.9.cloned.1.call-done = f32[8,4096]{1,0:T(8,128)} async-done(((f32[8,4096]{1,0:T(8,128)}), f32[8,4096]{1,0:T(8,128)}) %all-reduce.9.cloned.1.call-update) | async-done | bytes 131088 | tf_op jit(solution)/shard_map/psum | solution.py:75
  372.8 41.1 %all-reduce.7.cloned.1.call-done = f32[8,4096]{1,0:T(8,128)} async-done(((f32[8,4096]{1,0:T(8,128)}), f32[8,4096]{1,0:T(8,128)}) %all-reduce.7.cloned.1.call-update) | async-done | bytes 131088 | tf_op jit(solution)/shard_map/psum | solution.py:56
  413.9 0.8 fusion.31
  414.7 35.9 %all-gather = bf16[128,32,8]{1,2,0:T(8,128)(2,1)S(1)} all-gather(bf16[1,32,8]{1,2,0:T(8,128)(2,1)S(1)} %fusion.31), channel_id=1, replica_groups=mesh['leaf'=4,'rows'=32] {'leaf','rows'}, dimensions={0}, use_global_device_ids=true | all-gather | bytes 66048 | tf_op jit(solution)/shard_map/all_gather | solution.py:80
  450.6 0.3 reshape.142
  450.9 3.2 fusion.13
  454.1 0.0 all-reduce.11.cloned.1.call-update
  454.1 0.0 reduce-scatter.9.cloned.1.call-start
  454.2 98.7 %all-reduce.11.cloned.1.call-done = f32[8,4096]{1,0:T(8,128)} async-done(((f32[8,4096]{1,0:T(8,128)}), f32[8,4096]{1,0:T(8,128)}) %all-reduce.11.cloned.1.call-update) | async-done | bytes 131088 | tf_op jit(solution)/shard_map/psum | solution.py:85
  552.9 0.9 convert_element_type.36
  553.8 1.3 copy.71
  555.1 2.0 gather_fusion
  557.1 1.0 fusion.14
  558.1 0.0 reduce-scatter.11.cloned.1.call-start
  558.2 71.9 %reduce-scatter.9.cloned.1.call-done = f32[8,128]{1,0:T(8,128)} async-done(((f32[8,4096]{1,0:T(8,128)}), f32[8,128]{1,0:T(8,128)}) %reduce-scatter.9.cloned.1.call-update) | async-done | bytes 4112 | tf_op jit(solution)/shard_map/reduce_scatter | solution.py:91
  630.1 1.6 fusion.17
  631.7 0.0 reduce-scatter.13.cloned.1.call-start
  631.7 73.8 %reduce-scatter.11.cloned.1.call-done = f32[8,128]{1,0:T(8,128)} async-done(((f32[8,4096]{1,0:T(8,128)}), f32[8,128]{1,0:T(8,128)}) %reduce-scatter.11.cloned.1.call-update) | async-done | bytes 4112 | tf_op jit(solution)/shard_map/reduce_scatter | solution.py:94
  705.5 0.7 convert_element_type.38
  706.2 23.5 %all_gather.23 = bf16[8,4096]{1,0:T(8,128)(2,1)S(1)} all-gather(bf16[8,128]{1,0:T(8,128)(2,1)S(1)} %convert_element_type.38), channel_id=1, replica_groups=mesh['leaf'=4,'rows'=32] {'rows'}, dimensions={1}, use_global_device_ids=true | all-gather | bytes 67584 | tf_op jit(solution)/shard_map/all_gather | solution.py:95
  729.7 1.0 copy.72
  730.7 3.2 gather_fusion.1
  734.0 0.1 copy.73
  734.1 2.8 convolution_bitcast_fusion.1
  736.9 3.1 copy.76
  740.0 4.5 reshape.143
  744.6 0.0 reduce-scatter.15.cloned.1.call-start
  744.6 76.7 %reduce-scatter.13.cloned.1.call-done = f32[64,32]{1,0:T(8,128)} async-done(((f32[2048,32]{1,0:T(8,128)}), f32[64,32]{1,0:T(8,128)}) %reduce-scatter.13.cloned.1.call-update) | async-done | bytes 8208
  821.3 0.9 reshape.144
  822.2 0.1 copy.77
  822.3 0.3 convolution_bitcast_fusion
  822.6 3.1 copy.78
  825.6 4.5 reshape.145
  830.2 1.3 constant_dynamic-slice_fusion
  831.6 76.0 %reduce-scatter.15.cloned.1.call-done = f32[64,32]{1,0:T(8,128)} async-done(((f32[2048,32]{1,0:T(8,128)}), f32[64,32]{1,0:T(8,128)}) %reduce-scatter.15.cloned.1.call-update) | async-done | bytes 8208
  907.6 0.9 reshape.146
  908.5 0.7 copy.74
  (32 shorter events, 0.2 us)
Async XLA Ops:
  7.2 29.2 %copy-start = (bf16[4,64,2048]{2,1,0:T(8,128)(2,1)S(1)}, bf16[4,64,2048]{2,1,0:T(8,128)(2,1)}, u32[]{:S(2)}) copy-start(bf16[4,64,2048]{2,1,0:T(8,128)(2,1)} %param.15) | copy-start | bytes 3145732
  7.2 172.4 %all-reduce.5.cloned.1.call-start = ((), (), s32[]{:S(2)}) async-start(), calls=%async_computation.4 | async-start | bytes 524288 | tf_op jit(solution)/shard_map/psum | solution.py:54
  36.3 26.3 %copy-start.7 = (s32[4]{0:T(128)S(1)}, s32[4]{0:T(128)}, u32[]{:S(2)}) copy-start(s32[4]{0:T(128)} %param.18) | copy-start | bytes 52
  74.5 3.6 copy-start.8
  74.5 106.7 %copy-start.5 = (f32[8,1,128]{2,1,0:T(1,128)S(1)}, f32[8,1,128]{2,1,0:T(1,128)}, u32[]{:S(2)}) copy-start(f32[8,1,128]{2,1,0:T(1,128)} %param.13) | copy-start | bytes 12292
  74.5 131.4 %copy-start.3 = (bf16[1,128,4096]{2,1,0:T(8,128)(2,1)S(1)}, bf16[1,128,4096]{2,1,0:T(8,128)(2,1)}, u32[]{:S(2)}) copy-start(bf16[1,128,4096]{2,1,0:T(8,128)(2,1)} %param.19) | copy-start | bytes 3145732
  78.0 149.7 %copy-start.1 = (bf16[1,128,4096]{2,1,0:T(8,128)(2,1)S(1)}, bf16[1,128,4096]{2,1,0:T(8,128)(2,1)}, u32[]{:S(2)}) copy-start(bf16[1,128,4096]{2,1,0:T(8,128)(2,1)} %param.20) | copy-start | bytes 3145732
  78.1 294.8 %all-reduce.9.cloned.1.call-start = ((), (), s32[]{:S(2)}) async-start(), calls=%async_computation.6 | async-start | bytes 262144 | tf_op jit(solution)/shard_map/psum | solution.py:75
  228.2 185.7 %copy-start.6 = (f32[8,32]{1,0:T(8,128)S(1)}, f32[8,32]{1,0:T(8,128)}, u32[]{:S(2)}) copy-start(f32[8,32]{1,0:T(8,128)} %param.14) | copy-start | bytes 3076
  231.0 182.9 %all-reduce.7.cloned.1.call-start = ((), (), s32[]{:S(2)}) async-start(), calls=%async_computation.5 | async-start | bytes 262144 | tf_op jit(solution)/shard_map/psum | solution.py:56
  231.8 321.1 %all-reduce.11.cloned.1.call-start = ((), (), s32[]{:S(2)}) async-start(), calls=%async_computation.7 | async-start | bytes 262144 | tf_op jit(solution)/shard_map/psum | solution.py:85
  450.6 106.5 %copy-start.2 = (bf16[1,128,4096]{2,1,0:T(8,128)(2,1)S(1)}, bf16[1,128,4096]{2,1,0:T(8,128)(2,1)}, u32[]{:S(2)}) copy-start(bf16[1,128,4096]{2,1,0:T(8,128)(2,1)} %param.20) | copy-start | bytes 3145732
  450.9 179.2 %copy-start.4 = (bf16[1,128,4096]{2,1,0:T(8,128)(2,1)S(1)}, bf16[1,128,4096]{2,1,0:T(8,128)(2,1)}, u32[]{:S(2)}) copy-start(bf16[1,128,4096]{2,1,0:T(8,128)(2,1)} %param.19) | copy-start | bytes 3145732
  454.1 176.0 %reduce-scatter.9.cloned.1.call-start = ((), (), s32[]{:S(2)}) async-start(), calls=%async_computation.8 | async-start | bytes 135168 | tf_op jit(solution)/shard_map/reduce_scatter | solution.py:91
  558.1 147.3 %reduce-scatter.11.cloned.1.call-start = ((), (), s32[]{:S(2)}) async-start(), calls=%async_computation.9 | async-start | bytes 135168 | tf_op jit(solution)/shard_map/reduce_scatter | solution.py:94
  631.7 189.7 %reduce-scatter.13.cloned.1.call-start = ((), (), s32[]{:S(2)}) async-start(), calls=%async_computation.10 | async-start | bytes 1081344
  744.6 163.0 %reduce-scatter.15.cloned.1.call-start = ((), (), s32[]{:S(2)}) async-start(), calls=%async_computation.11 | async-start | bytes 1081344
Sparse Core Ops, SparseCore 0:
  78.2 101.3 all-reduce.4
  231.2 141.6 all-reduce.8
  375.1 38.7 all-reduce.6
  454.2 98.5 all-reduce.10
  558.3 71.7 reduce-scatter.8
  633.9 71.5 reduce-scatter.10
  744.7 76.6 reduce-scatter.12
  830.3 77.2 reduce-scatter.14
where the time goes:
time: 917 us; the launch traced here: 916 us
  waiting for transfers between devices  681 us (74%)
  blocking collectives  158 us (17%)
  local copies, waits for them, and re-layouts  35.6 us (4%)
  between operations  15 us (2%)
  matrix products  13.8 us (2%)
  other arithmetic  12.2 us (1%)
    unnamed x10, waiting for transfers between devices  154 us
    psum x1, waiting for transfers between devices, shards(): root_acc = root_from_leaves + lax.psum(parent_root, ('leaf', 'rows'))  141 us
    psum x1, waiting for transfers between devices, shards(): group_acc = lax.psum(local_acc, 'rows')  101 us
    psum x1, waiting for transfers between devices, shards(): root_full = lax.psum(root_term, 'rows')  98.7 us
    reduce_scatter x1, waiting for transfers between devices, shards(): lax.psum_scatter(parent_sol_term, 'rows', scatter_dimension=1, tiled=True)  73.8 us
    reduce_scatter x1, waiting for transfers between devices, shards(): lax.psum_scatter(parent_term, 'rows', scatter_dimension=1, tiled=True)  71.9 us
    psum x1, waiting for transfers between devices, shards(): root_from_leaves = lax.psum(group_acc[:, parent_width:], 'leaf')  41.1 us
    all_gather x1, blocking collectives, shards(): lax.all_gather(rrb, ('leaf', 'rows'), axis=1, tiled=True)  35.9 us
  transfers between devices with their start and end apart: 8, of which 8 were waited for; matrix products, arithmetic and copies ran while one was open for 0% of the time, Pallas kernels for 0%

commit v1 on v0

--- a/solution.py
+++ b/solution.py
@@ -82,7 +82,7 @@
         preferred_element_type=jnp.float32,
     )
     root_term = jnp.dot(ry.astype(jnp.bfloat16), root_inv, preferred_element_type=jnp.float32)
-    root_full = lax.psum(root_term, "rows")
+    root_full = jnp.sum(lax.all_gather(root_term, "rows"), axis=0)
     root_solution = lax.dynamic_slice_in_dim(root_full, flat_index * root_cols, root_cols, 1)
     rxb = root_full.astype(jnp.bfloat16)
     parent_anc = rxb[:, parent_rows[0]]

time: 917 us -> 865 us (0.943)
  waiting for transfers between devices: 681 us -> 626 us
    psum x1 -> x0, waiting for transfers between devices: 98.7 us -> none  [shards(): root_full = lax.psum(root_term, 'rows')]
    all_gather x0 -> x1, waiting for transfers between devices: none -> 43.7 us  [shards(): root_full = jnp.sum(lax.all_gather(root_term, 'rows'), axis=0)]
where the time goes in v1:
time: 865 us; the launch traced here: 864 us
  waiting for transfers between devices  626 us (72%)
  blocking collectives  158 us (18%)
  local copies, waits for them, and re-layouts  37 us (4%)
  between operations  15 us (2%)
  matrix products  13.8 us (2%)
  other arithmetic  13.7 us (2%)
    unnamed x10, waiting for transfers between devices  154 us
    psum x1, waiting for transfers between devices, shards(): root_acc = root_from_leaves + lax.psum(parent_root, ('leaf', 'rows'))  141 us
    psum x1, waiting for transfers between devices, shards(): group_acc = lax.psum(local_acc, 'rows')  101 us
    reduce_scatter x1, waiting for transfers between devices, shards(): lax.psum_scatter(parent_sol_term, 'rows', scatter_dimension=1, tiled=True)  73.8 us
    reduce_scatter x1, waiting for transfers between devices, shards(): lax.psum_scatter(parent_term, 'rows', scatter_dimension=1, tiled=True)  71.7 us
    all_gather x1, waiting for transfers between devices, shards(): root_full = jnp.sum(lax.all_gather(root_term, 'rows'), axis=0)  43.7 us
    psum x1, waiting for transfers between devices, shards(): root_from_leaves = lax.psum(group_acc[:, parent_width:], 'leaf')  41.1 us
    all_gather x1, blocking collectives, shards(): lax.all_gather(rrb, ('leaf', 'rows'), axis=1, tiled=True)  35.9 us
  transfers between devices with their start and end apart: 8, of which 8 were waited for; matrix products, arithmetic and copies ran while one was open for 0% of the time, Pallas kernels for 0%

profile of v1, /device:TPU:0, one launch (start us, length us, event | category | flops | bytes accessed | tf_op | source)
XLA Modules:
  0.0 864.3 jit_solution(8437186229718488752)
XLA Ops:
  7.2 0.0 all-reduce.4.cloned.1.call-start
  7.2 0.8 copy.81
  8.0 0.7 copy.91
  8.7 0.1 copy.62
  8.9 27.5 %all_gather.24 = bf16[8,4,2048]{0,1,2:T(4,128)(2,1)S(1)} all-gather(bf16[8,4,64]{0,1,2:T(4,128)(2,1)S(1)} %copy.62), channel_id=1, replica_groups=mesh['leaf'=4,'rows'=32] {'rows'}, dimensions={2}, use_global_device_ids=true | all-gather | bytes 135168 | tf_op jit(solution)/shard_map/all_gather | solution.py:33
  36.4 0.8 fusion.36
  37.1 0.1 copy.64
  37.3 25.3 %all_gather.25 = bf16[8,4,2048]{0,1,2:T(4,128)(2,1)S(1)} all-gather(bf16[8,4,64]{0,1,2:T(4,128)(2,1)S(1)} %copy.64), channel_id=1, replica_groups=mesh['leaf'=4,'rows'=32] {'rows'}, dimensions={2}, use_global_device_ids=true | all-gather | bytes 135168 | tf_op jit(solution)/shard_map/all_gather | solution.py:41
  62.6 0.1 broadcast_compare_fusion
  62.7 3.4 fusion.6
  66.1 0.2 copy.66
  66.3 8.2 scatter_custom_fusion
  74.5 3.5 copy.67
  78.0 0.0 all-reduce.4.cloned.1.call-update
  78.1 0.0 all-reduce.8.cloned.1.call-start
  78.9 100.7 %all-reduce.4.cloned.1.call-done = f32[8,8192]{1,0:T(8,128)} async-done(((f32[8,8192]{1,0:T(8,128)}), f32[8,8192]{1,0:T(8,128)}) %all-reduce.4.cloned.1.call-update) | async-done | bytes 262160 | tf_op jit(solution)/shard_map/psum | solution.py:54
  179.6 1.6 fusion.35
  181.2 24.6 %all_gather.26 = bf16[8,4096]{1,0:T(8,128)(2,1)S(1)} all-gather(bf16[8,128]{1,0:T(8,128)(2,1)S(1)} %subtract_convert_fusion.3), channel_id=1, replica_groups=mesh['leaf'=4,'rows'=32] {'rows'}, dimensions={1}, use_global_device_ids=true | all-gather | bytes 67584 | tf_op jit(solution)/shard_map/all_gather | solution.py:63
  205.9 0.4 fusion.37
  206.2 21.5 %all_gather.27 = bf16[8,4096]{1,0:T(8,128)(2,1)S(1)} all-gather(bf16[8,128]{1,0:T(8,128)(2,1)S(1)} %get-tuple-element.22), channel_id=1, replica_groups=mesh['leaf'=4,'rows'=32] {'rows'}, dimensions={1}, use_global_device_ids=true | all-gather | bytes 67584 | tf_op jit(solution)/shard_map/all_gather | solution.py:69
  227.8 0.4 fusion.12
  228.1 0.1 copy.68
  228.3 1.5 scatter_custom_fusion.1
  229.8 1.2 copy.69
  231.0 0.0 all-reduce.6.cloned.1.call-start
  231.1 0.7 all-reduce.6.cloned.1.call-update
  231.8 0.0 all-gather.4.cloned.1.call-start
  231.8 141.0 %all-reduce.8.cloned.1.call-done = f32[8,4096]{1,0:T(8,128)} async-done(((f32[8,4096]{1,0:T(8,128)}), f32[8,4096]{1,0:T(8,128)}) %all-reduce.8.cloned.1.call-update) | async-done | bytes 131088 | tf_op jit(solution)/shard_map/psum | solution.py:75
  372.8 41.1 %all-reduce.6.cloned.1.call-done = f32[8,4096]{1,0:T(8,128)} async-done(((f32[8,4096]{1,0:T(8,128)}), f32[8,4096]{1,0:T(8,128)}) %all-reduce.6.cloned.1.call-update) | async-done | bytes 131088 | tf_op jit(solution)/shard_map/psum | solution.py:56
  413.9 0.8 fusion.31
  414.7 35.9 %all-gather.1 = bf16[128,32,8]{1,2,0:T(8,128)(2,1)S(1)} all-gather(bf16[1,32,8]{1,2,0:T(8,128)(2,1)S(1)} %fusion.31), channel_id=1, replica_groups=mesh['leaf'=4,'rows'=32] {'leaf','rows'}, dimensions={0}, use_global_device_ids=true | all-gather | bytes 66048 | tf_op jit(solution)/shard_map/all_gather | solution.py:80
  450.6 0.3 reshape.143
  450.9 3.1 fusion.13
  454.0 0.0 all-gather.4.cloned.1.call-update
  454.0 0.0 reduce-scatter.9.cloned.1.call-start
  454.1 43.7 %all-gather.4.cloned.1.call-done = f32[256,4096]{1,0:T(8,128)} async-done(((f32[8,4096]{1,0:T(8,128)}), f32[256,4096]{1,0:T(8,128)}) %all-gather.4.cloned.1.call-update) | async-done | bytes 4194320 | tf_op jit(solution)/shard_map/all_gather | solution.py:85
  497.8 2.4 bitcast_reduce_fusion
  500.3 1.3 copy.71
  501.6 2.0 gather_fusion
  503.6 1.0 fusion.14
  504.6 0.0 reduce-scatter.11.cloned.1.call-start
  504.7 71.7 %reduce-scatter.9.cloned.1.call-done = f32[8,128]{1,0:T(8,128)} async-done(((f32[8,4096]{1,0:T(8,128)}), f32[8,128]{1,0:T(8,128)}) %reduce-scatter.9.cloned.1.call-update) | async-done | bytes 4112 | tf_op jit(solution)/shard_map/reduce_scatter | solution.py:91
  576.3 1.6 fusion.17
  577.9 0.0 reduce-scatter.13.cloned.1.call-start
  578.0 73.8 %reduce-scatter.11.cloned.1.call-done = f32[8,128]{1,0:T(8,128)} async-done(((f32[8,4096]{1,0:T(8,128)}), f32[8,128]{1,0:T(8,128)}) %reduce-scatter.11.cloned.1.call-update) | async-done | bytes 4112 | tf_op jit(solution)/shard_map/reduce_scatter | solution.py:94
  651.8 0.7 convert_element_type.38
  652.5 23.6 %all_gather.31 = bf16[8,4096]{1,0:T(8,128)(2,1)S(1)} all-gather(bf16[8,128]{1,0:T(8,128)(2,1)S(1)} %convert_element_type.38), channel_id=1, replica_groups=mesh['leaf'=4,'rows'=32] {'rows'}, dimensions={1}, use_global_device_ids=true | all-gather | bytes 67584 | tf_op jit(solution)/shard_map/all_gather | solution.py:95
  676.0 1.0 copy.72
  677.0 4.3 gather_fusion.1
  681.3 1.0 copy.73
  682.4 2.8 convolution_bitcast_fusion.1
  685.2 3.1 copy.76
  688.3 4.5 reshape.144
  692.9 0.0 reduce-scatter.15.cloned.1.call-start
  692.9 76.7 %reduce-scatter.13.cloned.1.call-done = f32[64,32]{1,0:T(8,128)} async-done(((f32[2048,32]{1,0:T(8,128)}), f32[64,32]{1,0:T(8,128)}) %reduce-scatter.13.cloned.1.call-update) | async-done | bytes 8208
  769.6 0.9 reshape.145
  770.5 0.1 copy.77
  770.6 0.3 convolution_bitcast_fusion
  770.8 3.1 copy.78
  773.9 4.5 reshape.146
  778.5 0.7 constant_dynamic-slice_fusion
  779.1 76.7 %reduce-scatter.15.cloned.1.call-done = f32[64,32]{1,0:T(8,128)} async-done(((f32[2048,32]{1,0:T(8,128)}), f32[64,32]{1,0:T(8,128)}) %reduce-scatter.15.cloned.1.call-update) | async-done | bytes 8208
  855.8 0.9 reshape.147
  856.7 0.7 copy.74
  (33 shorter events, 0.2 us)
Async XLA Ops:
  7.2 29.2 %copy-start = (bf16[4,64,2048]{2,1,0:T(8,128)(2,1)S(1)}, bf16[4,64,2048]{2,1,0:T(8,128)(2,1)}, u32[]{:S(2)}) copy-start(bf16[4,64,2048]{2,1,0:T(8,128)(2,1)} %param.15) | copy-start | bytes 3145732
  7.2 172.4 %all-reduce.4.cloned.1.call-start = ((), (), s32[]{:S(2)}) async-start(), calls=%async_computation.4 | async-start | bytes 524288 | tf_op jit(solution)/shard_map/psum | solution.py:54
  36.3 26.3 %copy-start.7 = (s32[4]{0:T(128)S(1)}, s32[4]{0:T(128)}, u32[]{:S(2)}) copy-start(s32[4]{0:T(128)} %param.18) | copy-start | bytes 52
  74.5 3.6 copy-start.8
  74.5 106.7 %copy-start.5 = (f32[8,1,128]{2,1,0:T(1,128)S(1)}, f32[8,1,128]{2,1,0:T(1,128)}, u32[]{:S(2)}) copy-start(f32[8,1,128]{2,1,0:T(1,128)} %param.13) | copy-start | bytes 12292
  74.5 131.4 %copy-start.3 = (bf16[1,128,4096]{2,1,0:T(8,128)(2,1)S(1)}, bf16[1,128,4096]{2,1,0:T(8,128)(2,1)}, u32[]{:S(2)}) copy-start(bf16[1,128,4096]{2,1,0:T(8,128)(2,1)} %param.19) | copy-start | bytes 3145732
  78.0 149.7 %copy-start.1 = (bf16[1,128,4096]{2,1,0:T(8,128)(2,1)S(1)}, bf16[1,128,4096]{2,1,0:T(8,128)(2,1)}, u32[]{:S(2)}) copy-start(bf16[1,128,4096]{2,1,0:T(8,128)(2,1)} %param.20) | copy-start | bytes 3145732
  78.1 294.8 %all-reduce.8.cloned.1.call-start = ((), (), s32[]{:S(2)}) async-start(), calls=%async_computation.6 | async-start | bytes 262144 | tf_op jit(solution)/shard_map/psum | solution.py:75
  228.2 185.7 %copy-start.6 = (f32[8,32]{1,0:T(8,128)S(1)}, f32[8,32]{1,0:T(8,128)}, u32[]{:S(2)}) copy-start(f32[8,32]{1,0:T(8,128)} %param.14) | copy-start | bytes 3076
  231.0 182.9 %all-reduce.6.cloned.1.call-start = ((), (), s32[]{:S(2)}) async-start(), calls=%async_computation.5 | async-start | bytes 262144 | tf_op jit(solution)/shard_map/psum | solution.py:56
  231.8 266.1 %all-gather.4.cloned.1.call-start = ((), (), s32[]{:S(2)}) async-start(), calls=%async_computation.9 | async-start | bytes 4325376 | tf_op jit(solution)/shard_map/all_gather | solution.py:85
  454.0 122.3 %reduce-scatter.9.cloned.1.call-start = ((), (), s32[]{:S(2)}) async-start(), calls=%async_computation.7 | async-start | bytes 135168 | tf_op jit(solution)/shard_map/reduce_scatter | solution.py:91
  454.1 49.5 %copy-start.2 = (bf16[1,128,4096]{2,1,0:T(8,128)(2,1)S(1)}, bf16[1,128,4096]{2,1,0:T(8,128)(2,1)}, u32[]{:S(2)}) copy-start(bf16[1,128,4096]{2,1,0:T(8,128)(2,1)} %param.20) | copy-start | bytes 3145732
  500.2 76.1 %copy-start.4 = (bf16[1,128,4096]{2,1,0:T(8,128)(2,1)S(1)}, bf16[1,128,4096]{2,1,0:T(8,128)(2,1)}, u32[]{:S(2)}) copy-start(bf16[1,128,4096]{2,1,0:T(8,128)(2,1)} %param.19) | copy-start | bytes 3145732
  504.6 147.1 %reduce-scatter.11.cloned.1.call-start = ((), (), s32[]{:S(2)}) async-start(), calls=%async_computation.8 | async-start | bytes 135168 | tf_op jit(solution)/shard_map/reduce_scatter | solution.py:94
  577.9 191.6 %reduce-scatter.13.cloned.1.call-start = ((), (), s32[]{:S(2)}) async-start(), calls=%async_computation.10 | async-start | bytes 1081344
  692.9 163.0 %reduce-scatter.15.cloned.1.call-start = ((), (), s32[]{:S(2)}) async-start(), calls=%async_computation.11 | async-start | bytes 1081344
Sparse Core Ops, SparseCore 0:
  78.2 101.3 all-reduce.3
  231.2 141.6 all-reduce.7
  375.1 38.7 all-reduce.5
  454.1 43.6 all-gather.3
  504.8 71.5 reduce-scatter.8
  580.2 71.5 reduce-scatter.10
  693.0 76.5 reduce-scatter.12
  778.6 77.1 reduce-scatter.14
